TPU v7x, 256 devices: a whole 4x4x8 slice. The times are simulated.
256 devices in a mesh: row: 8 (over y, core), col: 32 (over x, z).
Axes of the slice: x: 4, y: 4, z: 8, core: 2. Of those that a mesh axis runs over, the one named last changes fastest.
Arguments:
- tokens: bfloat16 [16384, 3072], P(('row', 'col')), may hold values from -6 to 6
- w_in: bfloat16 [3072, 12288], P('row', 'col'), may hold values from -0.109375 to 0.109375
- b_in: float32 [12288], P('col'), may hold values from -3 to 3
- conv_taps: float32 [27, 12288], P(None, 'col'), may hold values from -1.25 to 1.25
- conv_bias: float32 [12288], P('col'), may hold values from -3 to 3
- w_out: bfloat16 [12288, 3072], P('col', 'row'), may hold values from -0.0546875 to 0.0546875
- b_out: float32 [3072], replicated, may hold values from -3 to 3
Outputs:
- mixed: bfloat16 [16384, 3072], P(('row', 'col'))
All inputs are finite; a program needn't handle non-finite values.
Results may differ from a plain program's by a relative error of at most 0.0053.
Values may be sent and summed in bfloat16 or wider, within the bound.
A program may use at most 128 MiB of HBM per device.

v0:
```python
import jax
import jax.numpy as jnp
from jax import lax
from jax.sharding import PartitionSpec as P

HH = 32
WW = 32


def with_halo(shard, sides, width):
    for axis, dim in sides:
        count, length = (lax.axis_size(axis), shard.shape[dim])
        up = [(i, (i + 1) % count) for i in range(count - 1)]
        down = [(j, i) for i, j in up]
        last = lax.slice_in_dim(shard, length - width, length, axis=dim)
        initial = lax.slice_in_dim(shard, 0, width, axis=dim)
        before = lax.ppermute(last, axis, up)
        after = lax.ppermute(initial, axis, down)
        shard = jnp.concatenate([before, shard, after], axis=dim)
    return shard


def body(tokens, w_in, b_in, conv_taps, conv_bias, w_out, b_out):
    own_rows = tokens.shape[0]
    tok_rows = own_rows * lax.axis_size("col")
    hid_cols = w_in.shape[1]
    frame_count = tok_rows // (HH * WW)
    whole = lax.all_gather(tokens, "col", axis=0, tiled=True)
    before = jnp.dot(
        whole, lax.all_gather(w_in, "row", axis=0, tiled=True), preferred_element_type=jnp.float32
    )
    hidden = (before + b_in).astype(jnp.bfloat16).reshape(frame_count, HH, WW, hid_cols)
    extended = with_halo(hidden, (("row", 0),), 1)
    padded = jnp.pad(extended, ((0, 0), (1, 1), (1, 1), (0, 0)))
    summed = jnp.zeros((frame_count, HH, WW, hid_cols), jnp.float32)
    for offset in range(27):
        shift_t = offset // 9
        shift_h = offset // 3 % 3
        shift_w = offset % 3
        window = padded[
            shift_t : shift_t + frame_count, shift_h : shift_h + HH, shift_w : shift_w + WW, :
        ]
        summed = summed + window.astype(jnp.float32) * conv_taps[offset]
    activated = jax.nn.gelu(summed + conv_bias, approximate=True).astype(jnp.bfloat16)
    activated = activated.reshape(tok_rows, hid_cols)
    partial_value = jnp.dot(
        activated,
        lax.all_gather(w_out, "row", axis=1, tiled=True),
        preferred_element_type=jnp.float32,
    )
    shares = lax.psum_scatter(partial_value, "col", scatter_dimension=0, tiled=True)
    return (shares + b_out).astype(jnp.bfloat16)


def solution(mesh):
    placed = (
        P(("row", "col"), None),
        P("row", "col"),
        P("col"),
        P(None, "col"),
        P("col"),
        P("col", "row"),
        P(),
    )
    return jax.shard_map(
        body, mesh=mesh, in_specs=placed, out_specs=P(("row", "col"), None), check_vma=False
    )
```

profile of v0, /device:TPU:16, one launch (start us, length us, event | category | flops | bytes accessed | tf_op | source)
XLA Modules:
  0.0 494.6 jit_solution(7462746669944708098)
XLA Ops:
  6.5 0.0 all-gather.6.cloned.1.call-start
  6.5 0.7 all-gather.6.cloned.1.call-update
  7.3 0.0 all-gather.4.cloned.1.call-start
  7.3 0.7 all-gather.4.cloned.1.call-update
  8.0 0.0 all-gather.8.cloned.1.call-start
  8.1 31.4 %all-gather.6.cloned.1.call-done = bf16[3072,384]{1,0:T(8,128)(2,1)} async-done(((bf16[384,384]{1,0:T(8,128)(2,1)}), bf16[3072,384]{1,0:T(8,128)(2,1)}) %all-gather.6.cloned.1.call-update) | async-done | bytes 2359312 | tf_op jit(solution)/shard_map/all_gather | solution.py:30
  39.4 122.6 %all-gather.4.cloned.1.call-done = bf16[2048,3072]{1,0:T(8,128)(2,1)} async-done(((bf16[64,3072]{1,0:T(8,128)(2,1)}), bf16[2048,3072]{1,0:T(8,128)(2,1)}) %all-gather.4.cloned.1.call-update) | async-done | bytes 12582928 | tf_op jit(solution)/shard_map/all_gather | solution.py:28
  162.0 10.4 %add_convert_fusion = bf16[2048,384]{1,0:T(8,128)(2,1)S(1)} fusion(bf16[2048,3072]{1,0:T(8,128)(2,1)} %all-gather.4.cloned.1.call-done, bf16[3072,384]{1,0:T(8,128)(2,1)} %all-gather.6.cloned.1.call-done, f32[384]{0:T(512)} %param.9), kind=kOutput, calls=%fused_computation.21 | convolution fusion | flops 4833411072 | bytes 16516608 | tf_op jit(solution)/shard_map/dot_general | solution.py:29
  172.4 0.0 copy-start.2
  172.4 1.3 fusion.14
  173.7 1.9 collective-permute-start.1
  175.6 2.4 collective-permute-start
  178.1 0.0 all-gather.8.cloned.1.call-update
  178.1 0.0 reduce-scatter.2.cloned.1.call-start
  178.1 0.0 copy-done.2
  178.2 0.1 slice_reduce_fusion.26
  178.3 7.2 %collective-permute-done.1 = bf16[1,32,32,384]{3,2,1,0:T(8,128)(2,1)S(1)} collective-permute-done((bf16[1,32,32,384]{3,2,1,0:T(8,128)(2,1)}, bf16[1,32,32,384]{3,2,1,0:T(8,128)(2,1)S(1)}, u32[]{:S(2)}, u32[]{:S(2)}) %collective-permute-start.1) | collective-permute-done | bytes 786464 | tf_op jit(solution)/shard_map/ppermute | solution.py:18
  185.4 0.0 copy-start
  185.4 3.7 collective-permute-done
  189.2 0.0 copy-start.1
  189.2 0.0 copy-start.4
  189.2 1.9 select_maximum_fusion
  191.1 0.0 copy-done
  191.1 0.0 copy-done.1
  191.1 0.0 copy-done.4
  191.1 14.5 %fusion.13 = bf16[2,32,32,384]{3,2,1,0:T(8,128)(2,1)S(1)} fusion(bf16[2,32,32,384]{3,2,1,0:T(8,128)(2,1)S(1)} %bitcast.9, bf16[4,34,34,384]{3,2,1,0:T(8,128)(2,1)S(1)} %select_maximum_fusion, bf16[1,32,32,384]{3,2,1,0:T(8,128)(2,1)} %copy-done, bf16[1,32,32,384]{3,2,1,0:T(8,128)(2,1)} %copy-done.1, f32[384]{0:T(512)S(1)} %copy-done.4, ...), kind=kLoop, calls=%fused_computation.20 | loop fusion | flops 72351744 | bytes 42510336 | tf_op jit(solution)/shard_map/convert_element_type | solution.py:44
  205.6 0.0 all-gather.8.cloned.1.call-done
  205.6 13.3 %fusion.15 = f32[2048,3072]{1,0:T(8,128)} fusion(bf16[2048,384]{1,0:T(8,128)(2,1)S(1)} %bitcast.10, bf16[384,3072]{1,0:T(8,128)(2,1)} %all-gather.8.cloned.1.call-done), kind=kOutput, calls=%fused_computation.53 | convolution fusion | flops 4831838208 | bytes 29097984 | tf_op jit(solution)/shard_map/dot_general | solution.py:46
  219.0 0.0 copy-start.3
  219.0 0.0 reduce-scatter.2.cloned.1.call-update
  219.0 267.2 %reduce-scatter.2.cloned.1.call-done = f32[64,3072]{1,0:T(8,128)} async-done(((f32[2048,3072]{1,0:T(8,128)}), f32[64,3072]{1,0:T(8,128)}) %reduce-scatter.2.cloned.1.call-update) | async-done | bytes 786448 | tf_op jit(solution)/shard_map/reduce_scatter | solution.py:51
  486.2 0.0 copy-done.3
  486.2 1.9 add_convert_fusion.1
  (1 shorter events, 0.0 us)
Async XLA Ops:
  6.5 32.9 %all-gather.6.cloned.1.call-start = ((), (), s32[]{:S(2)}) async-start(), calls=%async_computation.2 | async-start | bytes 2654208 | tf_op jit(solution)/shard_map/all_gather | solution.py:30
  7.3 154.7 %all-gather.4.cloned.1.call-start = ((), (), s32[]{:S(2)}) async-start(), calls=%async_computation.1 | async-start | bytes 12976128 | tf_op jit(solution)/shard_map/all_gather | solution.py:28
  8.0 197.6 %all-gather.8.cloned.1.call-start = ((), (), s32[]{:S(2)}) async-start(), calls=%async_computation.3 | async-start | bytes 2654208 | tf_op jit(solution)/shard_map/all_gather | solution.py:48
  172.4 5.7 %copy-start.2 = (f32[27,384]{1,0:T(8,128)S(1)}, f32[27,384]{1,0:T(8,128)}, u32[]{:S(2)}) copy-start(f32[27,384]{1,0:T(8,128)} %param.10) | copy-start | bytes 124420
  173.7 11.7 %collective-permute-start.1 = (bf16[1,32,32,384]{3,2,1,0:T(8,128)(2,1)}, bf16[1,32,32,384]{3,2,1,0:T(8,128)(2,1)S(1)}, u32[]{:S(2)}, u32[]{:S(2)}) collective-permute-start(bf16[1,32,32,384]{3,2,1,0:T(8,128)(2,1)} %bitcast.2), channel_id=1, source_target_pairs={{32,0},{64,32},{96,64},{128,96},{160,128},{192,160},{224,192},{33,... | collective-permute-start | bytes 2359304 | tf_op jit(solution)/shard_map/ppermute | solution.py:18
  175.6 13.5 %collective-permute-start = (bf16[1,32,32,384]{3,2,1,0:T(8,128)(2,1)}, bf16[1,32,32,384]{3,2,1,0:T(8,128)(2,1)S(1)}, u32[]{:S(2)}, u32[]{:S(2)}) collective-permute-start(bf16[1,32,32,384]{3,2,1,0:T(8,128)(2,1)} %bitcast), channel_id=1, source_target_pairs={{0,32},{32,64},{64,96},{96,128},{128,160},{160,192},{192,224},{1,3... | collective-permute-start | bytes 2359304 | tf_op jit(solution)/shard_map/ppermute | solution.py:17
  178.1 308.1 %reduce-scatter.2.cloned.1.call-start = ((), (), s32[]{:S(2)}) async-start(), calls=%async_computation.4 | async-start | bytes 25952256 | tf_op jit(solution)/shard_map/reduce_scatter | solution.py:51
  185.4 5.6 %copy-start = (bf16[1,32,32,384]{3,2,1,0:T(8,128)(2,1)}, bf16[1,32,32,384]{3,2,1,0:T(8,128)(2,1)S(1)}, u32[]{:S(2)}) copy-start(bf16[1,32,32,384]{3,2,1,0:T(8,128)(2,1)S(1)} %collective-permute-done.1) | copy-start | bytes 2359300
  189.2 1.9 copy-start.1
  189.2 1.9 copy-start.4
  219.0 267.2 %copy-start.3 = (f32[3072]{0:T(1024)S(1)}, f32[3072]{0:T(1024)}, u32[]{:S(2)}) copy-start(f32[3072]{0:T(1024)} %param.13) | copy-start | bytes 36868
Sparse Core Ops, SparseCore 0:
  9.2 30.2 all-gather.5
  42.0 119.9 all-gather.3
  178.2 25.0 all-gather.7
  219.1 267.0 reduce-scatter.1
where the time goes:
time: 495 us
  waiting for transfers between devices  433 us (87%)
  matrix products  23.7 us (5%)
  other arithmetic  18.3 us (4%)
  between operations  13.2 us (3%)
    reduce_scatter x1, waiting for transfers between devices, body(): lax.psum_scatter(partial_value, 'col', scatter_dimension=0, tiled=True)  267 us
    all_gather x1, waiting for transfers between devices, body(): whole = lax.all_gather(tokens, 'col', axis=0, tiled=True)  123 us
    all_gather x1, waiting for transfers between devices, body(): lax.all_gather(w_in, 'row', axis=0, tiled=True)  31.4 us
    convert_element_type x1, other arithmetic, body(): jax.nn.gelu(summed + conv_bias, approximate=True).astype(jnp.bfloat16)  14.5 us
    dot_general x1, matrix products, body(): jnp.dot(activated, lax.all_gather(w_out, 'row', axis=1, tiled=True), pref...  13.3 us
    dot_general x1, matrix products, body(): jnp.dot(whole, lax.all_gather(w_in, 'row', axis=0, tiled=True), preferred...  10.4 us
  transfers between devices with their start and end apart: 6, of which 5 were waited for; matrix products, arithmetic and copies ran while one was open for 3% of the time, Pallas kernels for 0%

commit v1 on v0

--- a/solution.py
+++ b/solution.py
@@ -25,7 +25,9 @@
     tok_rows = own_rows * lax.axis_size("col")
     hid_cols = w_in.shape[1]
     frame_count = tok_rows // (HH * WW)
-    whole = lax.all_gather(tokens, "col", axis=0, tiled=True)
+    whole = jnp.concatenate(
+        lax.all_to_all(jnp.stack([tokens] * lax.axis_size("col")), "col", 0, 0), axis=0
+    )
     before = jnp.dot(
         whole, lax.all_gather(w_in, "row", axis=0, tiled=True), preferred_element_type=jnp.float32
     )

time: 495 us -> 660 us (1.33)
  waiting for transfers between devices: 433 us -> 579 us
  starting transfers between devices: 4.43 us -> 17.2 us
  local copies, waits for them, and re-layouts: 1.48 us -> 8.58 us
    all_to_all x0 -> x1, waiting for transfers between devices: none -> 250 us  [body(): lax.all_to_all(jnp.stack([tokens] * lax.axis_size('col')), 'col', 0, 0)]
    all_gather x1 -> x0, waiting for transfers between devices: 123 us -> none  [body(): whole = lax.all_gather(tokens, 'col', axis=0, tiled=True)]
    all_gather x1, waiting for transfers between devices: 0.02 us -> 18.3 us  [body(): lax.all_gather(w_out, 'row', axis=1, tiled=True)]
    all_to_all x0 -> x1, starting transfers between devices: none -> 11.6 us  [body(): lax.all_to_all(jnp.stack([tokens] * lax.axis_size('col')), 'col', 0, 0)]
    another operation x0 -> x1, local copies, waits for them, and re-layouts: none -> 7.07 us  [body(): jnp.stack([tokens] * lax.axis_size('col'))]
  transfers between devices with their start and end apart: 6 -> 6, of which waited for: 5 -> 6; matrix products, arithmetic and copies ran while one was open for 3% -> 3% of each run, Pallas kernels for 0% -> 0%
where the time goes in v1:
time: 660 us
  waiting for transfers between devices  579 us (88%)
  matrix products  23.7 us (4%)
  other arithmetic  18.3 us (3%)
  starting transfers between devices  17.2 us (3%)
  between operations  13.2 us (2%)
  local copies, waits for them, and re-layouts  8.58 us (1%)
    reduce_scatter x1, waiting for transfers between devices, body(): lax.psum_scatter(partial_value, 'col', scatter_dimension=0, tiled=True)  270 us
    all_to_all x1, waiting for transfers between devices, body(): lax.all_to_all(jnp.stack([tokens] * lax.axis_size('col')), 'col', 0, 0)  250 us
    all_gather x1, waiting for transfers between devices, body(): lax.all_gather(w_in, 'row', axis=0, tiled=True)  30.5 us
    all_gather x1, waiting for transfers between devices, body(): lax.all_gather(w_out, 'row', axis=1, tiled=True)  18.3 us
    convert_element_type x1, other arithmetic, body(): jax.nn.gelu(summed + conv_bias, approximate=True).astype(jnp.bfloat16)  14.5 us
    dot_general x1, matrix products, body(): jnp.dot(activated, lax.all_gather(w_out, 'row', axis=1, tiled=True), pref...  13.3 us
  transfers between devices with their start and end apart: 6, of which 6 were waited for; matrix products, arithmetic and copies ran while one was open for 3% of the time, Pallas kernels for 0%

profile of v1, /device:TPU:16, one launch (start us, length us, event | category | flops | bytes accessed | tf_op | source)
XLA Modules:
  0.0 660.0 jit_solution(1650704989009734922)
XLA Ops:
  6.5 7.1 %stack.2 = bf16[32,64,3072]{2,1,0:T(8,128)(2,1)} broadcast(bf16[64,3072]{1,0:T(8,128)(2,1)} %param.7), dimensions={1,2} | broadcast | bytes 12976128 | tf_op jit(solution)/shard_map/stack | solution.py:29
  13.6 0.0 copy-start.5
  13.6 11.6 %all-to-all-start = ((bf16[32,64,3072]{2,1,0:T(8,128)(2,1)}), bf16[32,64,3072]{2,1,0:T(8,128)(2,1)}, u32[]{:S(2)}, u32[]{:S(2)}) async-start(bf16[32,64,3072]{2,1,0:T(8,128)(2,1)} %stack.2), calls=%async_computation | async-start | bytes 25165824 | tf_op jit(solution)/shard_map/all_to_all | solution.py:29
  25.2 0.0 all-gather.3.cloned.1.call-start
  25.2 0.7 all-gather.3.cloned.1.call-update
  25.9 0.0 all-gather.5.cloned.1.call-start
  26.0 30.5 %all-gather.3.cloned.1.call-done = bf16[3072,384]{1,0:T(8,128)(2,1)} async-done(((bf16[384,384]{1,0:T(8,128)(2,1)}), bf16[3072,384]{1,0:T(8,128)(2,1)}) %all-gather.3.cloned.1.call-update) | async-done | bytes 2359312 | tf_op jit(solution)/shard_map/all_gather | solution.py:32
  56.5 249.7 %all-to-all-done = bf16[32,64,3072]{2,1,0:T(8,128)(2,1)} async-done(((bf16[32,64,3072]{2,1,0:T(8,128)(2,1)}), bf16[32,64,3072]{2,1,0:T(8,128)(2,1)}, u32[]{:S(2)}, u32[]{:S(2)}) %all-to-all-start) | async-done | bytes 12582944 | tf_op jit(solution)/shard_map/all_to_all | solution.py:29
  306.2 0.0 copy-done.5
  306.2 10.4 %add_convert_fusion = bf16[2048,384]{1,0:T(8,128)(2,1)S(1)} fusion(bf16[2048,3072]{1,0:T(8,128)(2,1)} %bitcast, bf16[3072,384]{1,0:T(8,128)(2,1)} %all-gather.3.cloned.1.call-done, f32[384]{0:T(512)S(1)} %copy-done.5), kind=kOutput, calls=%fused_computation.21 | convolution fusion | flops 4833411072 | bytes 16516608 | tf_op jit(solution)/shard_map/dot_general | solution.py:31
  316.6 0.0 copy-start.2
  316.6 1.3 fusion.14
  317.9 1.9 collective-permute-start
  319.8 3.6 collective-permute-start.1
  323.5 0.0 all-gather.5.cloned.1.call-update
  323.5 0.0 reduce-scatter.2.cloned.1.call-start
  323.6 0.0 copy-done.2
  323.6 0.1 slice_reduce_fusion.26
  323.7 7.7 %collective-permute-done = bf16[1,32,32,384]{3,2,1,0:T(8,128)(2,1)S(1)} collective-permute-done((bf16[1,32,32,384]{3,2,1,0:T(8,128)(2,1)}, bf16[1,32,32,384]{3,2,1,0:T(8,128)(2,1)S(1)}, u32[]{:S(2)}, u32[]{:S(2)}) %collective-permute-start) | collective-permute-done | bytes 786464 | tf_op jit(solution)/shard_map/ppermute | solution.py:17
  331.4 0.0 copy-start
  331.4 1.9 collective-permute-done.1
  333.3 0.0 copy-start.1
  333.3 0.0 copy-start.4
  333.3 1.9 select_maximum_fusion
  335.2 0.0 copy-done
  335.2 0.0 copy-done.1
  335.2 0.0 copy-done.4
  335.2 14.5 %fusion.13 = bf16[2,32,32,384]{3,2,1,0:T(8,128)(2,1)S(1)} fusion(bf16[2,32,32,384]{3,2,1,0:T(8,128)(2,1)S(1)} %bitcast.10, bf16[4,34,34,384]{3,2,1,0:T(8,128)(2,1)S(1)} %select_maximum_fusion, bf16[1,32,32,384]{3,2,1,0:T(8,128)(2,1)} %copy-done.1, bf16[1,32,32,384]{3,2,1,0:T(8,128)(2,1)} %copy-done, f32[384]{0:T(512)S(1)} %copy-done.4, ...), kind=kLoop, calls=%fused_computation.20 | loop fusion | flops 72351744 | bytes 42510336 | tf_op jit(solution)/shard_map/convert_element_type | solution.py:46
  349.7 18.3 %all-gather.5.cloned.1.call-done = bf16[384,3072]{1,0:T(8,128)(2,1)} async-done(((bf16[384,384]{1,0:T(8,128)(2,1)}), bf16[384,3072]{1,0:T(8,128)(2,1)}) %all-gather.5.cloned.1.call-update) | async-done | bytes 2359312 | tf_op jit(solution)/shard_map/all_gather | solution.py:50
  368.0 13.3 %fusion.15 = f32[2048,3072]{1,0:T(8,128)} fusion(bf16[2048,384]{1,0:T(8,128)(2,1)S(1)} %bitcast.11, bf16[384,3072]{1,0:T(8,128)(2,1)} %all-gather.5.cloned.1.call-done), kind=kOutput, calls=%fused_computation.53 | convolution fusion | flops 4831838208 | bytes 29097984 | tf_op jit(solution)/shard_map/dot_general | solution.py:48
  381.3 0.0 copy-start.3
  381.4 0.0 reduce-scatter.2.cloned.1.call-update
  381.4 270.2 %reduce-scatter.2.cloned.1.call-done = f32[64,3072]{1,0:T(8,128)} async-done(((f32[2048,3072]{1,0:T(8,128)}), f32[64,3072]{1,0:T(8,128)}) %reduce-scatter.2.cloned.1.call-update) | async-done | bytes 786448 | tf_op jit(solution)/shard_map/reduce_scatter | solution.py:53
  651.6 0.0 copy-done.3
  651.6 1.9 add_convert_fusion.1
  (1 shorter events, 0.0 us)
Async XLA Ops:
  13.6 292.6 %copy-start.5 = (f32[384]{0:T(512)S(1)}, f32[384]{0:T(512)}, u32[]{:S(2)}) copy-start(f32[384]{0:T(512)} %param.9) | copy-start | bytes 4612
  13.6 292.6 %all-to-all-start = ((bf16[32,64,3072]{2,1,0:T(8,128)(2,1)}), bf16[32,64,3072]{2,1,0:T(8,128)(2,1)}, u32[]{:S(2)}, u32[]{:S(2)}) async-start(bf16[32,64,3072]{2,1,0:T(8,128)(2,1)} %stack.2), calls=%async_computation | async-start | bytes 25165824 | tf_op jit(solution)/shard_map/all_to_all | solution.py:29
  25.2 31.3 %all-gather.3.cloned.1.call-start = ((), (), s32[]{:S(2)}) async-start(), calls=%async_computation.2 | async-start | bytes 2654208 | tf_op jit(solution)/shard_map/all_gather | solution.py:32
  25.9 342.1 %all-gather.5.cloned.1.call-start = ((), (), s32[]{:S(2)}) async-start(), calls=%async_computation.3 | async-start | bytes 2654208 | tf_op jit(solution)/shard_map/all_gather | solution.py:50
  316.6 7.0 %copy-start.2 = (f32[27,384]{1,0:T(8,128)S(1)}, f32[27,384]{1,0:T(8,128)}, u32[]{:S(2)}) copy-start(f32[27,384]{1,0:T(8,128)} %param.10) | copy-start | bytes 124420
  317.9 13.5 %collective-permute-start = (bf16[1,32,32,384]{3,2,1,0:T(8,128)(2,1)}, bf16[1,32,32,384]{3,2,1,0:T(8,128)(2,1)S(1)}, u32[]{:S(2)}, u32[]{:S(2)}) collective-permute-start(bf16[1,32,32,384]{3,2,1,0:T(8,128)(2,1)} %bitcast.1), channel_id=1, source_target_pairs={{0,32},{32,64},{64,96},{96,128},{128,160},{160,192},{192,224},{1,3... | collective-permute-start | bytes 2359304 | tf_op jit(solution)/shard_map/ppermute | solution.py:17
  319.8 13.5 %collective-permute-start.1 = (bf16[1,32,32,384]{3,2,1,0:T(8,128)(2,1)}, bf16[1,32,32,384]{3,2,1,0:T(8,128)(2,1)S(1)}, u32[]{:S(2)}, u32[]{:S(2)}) collective-permute-start(bf16[1,32,32,384]{3,2,1,0:T(8,128)(2,1)} %bitcast.3), channel_id=1, source_target_pairs={{32,0},{64,32},{96,64},{128,96},{160,128},{192,160},{224,192},{33,... | collective-permute-start | bytes 2359304 | tf_op jit(solution)/shard_map/ppermute | solution.py:18
  323.5 328.1 %reduce-scatter.2.cloned.1.call-start = ((), (), s32[]{:S(2)}) async-start(), calls=%async_computation.4 | async-start | bytes 25952256 | tf_op jit(solution)/shard_map/reduce_scatter | solution.py:53
  331.4 3.8 copy-start
  333.3 1.9 copy-start.1
  333.3 1.9 copy-start.4
  381.3 270.2 %copy-start.3 = (f32[3072]{0:T(1024)S(1)}, f32[3072]{0:T(1024)}, u32[]{:S(2)}) copy-start(f32[3072]{0:T(1024)} %param.13) | copy-start | bytes 36868
Sparse Core Ops, SparseCore 0:
  27.8 28.6 all-gather.2
  323.6 44.3 all-gather.4
  381.5 270.0 reduce-scatter.1
